TPU v7x, 32 devices: a whole 2x2x4 slice. The times are simulated.
32 devices in a mesh: grp: 2 (over y), row: 4 (over x, core), col: 4 (over z).
Axes of the slice: x: 2, y: 2, z: 4, core: 2. Of those that a mesh axis runs over, the one named last changes fastest.
Arguments:
- factor: float32 [8, 4, 768, 768], P(('grp', 'row'), 'col'), parts along dimension 0
- rhs: float32 [8, 768, 64], P(('grp', 'row')), parts along dimension 0, may hold values from -6 to 6
- pattern: int32 [8, 4], P('grp'), parts along dimension 0, may hold values from 0 to 1, as said below
Outputs:
- solution: float32 [8, 768, 64], P(('grp', 'col'), 'row'), parts along dimension 0
There are 2 independent parts, one for each index of `grp`. A program takes and returns all parts, laid end to end along the dimension named above; each array names one. Nothing has to cross between parts.
Inputs may be any that keep to these rules, and one draw needn't show every extreme that they name: pattern[i, j] = 1 only where j < i; the blocks form an elimination tree in which every block but the last has exactly one parent p > j with pattern[p, j] = 1, and pattern[i, j] = 1 only where i is an ancestor of j; every chain of blocks linked by pattern has at most 4 blocks and some chain has exactly 4.
All inputs are finite; a program needn't handle non-finite values.
Results may differ from a plain program's by a relative error of at most 0.0001.
Values sent between devices are 32-bit elements; how exact they have to be, the bound alone decides.
A program may use at most 64 MiB of HBM per device.

v0:
```python
import jax
import jax.numpy as jnp
from jax import lax
from jax.sharding import PartitionSpec as P


def from_root(shard, axis, root):
    mine = lax.axis_index(axis) == root
    return lax.psum(jnp.where(mine, shard, jnp.zeros_like(shard)), axis)


def multiply(factor_tile, columns):
    return jnp.dot(
        factor_tile, columns, precision=lax.Precision.HIGHEST, preferred_element_type=jnp.float32
    )


def advance(factor_tile, right_cols, carried, solve_now, apply_now, final_level):

    def solve_branch(operand):
        return multiply(factor_tile, operand)

    def empty_branch(operand):
        return jnp.zeros_like(operand)

    fresh = lax.cond(solve_now, solve_branch, empty_branch, right_cols - carried)
    arrived = from_root(fresh, "row", lax.axis_index("col"))
    if not final_level:
        product = lax.cond(apply_now, solve_branch, empty_branch, arrived)
        carried = carried + lax.psum(product, "col")
    return (arrived, carried)


def local(factor, rhs, pattern):
    factor_tile = factor[0, 0]
    right_rows = rhs[0]
    here_row = lax.axis_index("row")
    here_col = lax.axis_index("col")
    depth_count = min(6, lax.axis_size("row"))
    linked = pattern == 1
    height = jnp.zeros((pattern.shape[0],), jnp.int32)
    for sweep_index in range(depth_count):
        height = jnp.max(jnp.where(linked, height[None, :] + 1, 0), axis=1)
    own_height = height[here_row]
    column_height = height[here_col]
    on_diagonal = here_row == here_col
    uses_block = pattern[here_row, here_col] == 1
    pieces = [right_rows]
    carried = [jnp.zeros_like(piece) for piece in pieces]
    solved = [jnp.zeros_like(piece) for piece in pieces]
    for level_now in range(depth_count):
        solve_now = on_diagonal & (own_height == level_now)
        apply_now = uses_block & (column_height == level_now)
        arrived, carried[0] = advance(
            factor_tile, pieces[0], carried[0], solve_now, apply_now, level_now == depth_count - 1
        )
        solved[0] = solved[0] + arrived
    solved_all = solved[0]
    own_rows = solved_all.shape[0] // lax.axis_size("row")
    return lax.dynamic_slice_in_dim(solved_all, here_row * own_rows, own_rows, 0)[None]


def solution(mesh):
    in_specs = (P(("grp", "row"), "col", None, None), P(("grp", "row"), None, None), P("grp", None))
    out_specs = P(("grp", "col"), "row", None)
    return jax.shard_map(local, mesh=mesh, in_specs=in_specs, out_specs=out_specs, check_vma=False)
```

profile of v0, /device:TPU:0, one launch (start us, length us, event | category | flops | bytes accessed | tf_op | source)
XLA Modules:
  0.0 278.0 jit_solution(16955222185634692702)
XLA Ops:
  6.5 0.8 select_reduce_fusion.3
  7.3 0.1 select_reduce_fusion.2
  7.7 0.6 fusion.5
  9.0 1.1 copy.4
  10.1 3.8 %conditional.7 = (f32[768,64]{0,1:T(8,128)S(1)}) conditional(s32[]{:T(128)} %convert_element_type.21, () %tuple.47, (f32[768,768]{1,0:T(8,128)}, f32[768,64]{1,0:T(8,128)S(1)}) %tuple.101), branch_computations={%region_4.5_spmd, %region_5.6_spmd} | conditional | flops 452984832 | bytes 2752520 | solution.py:26
  10.1 3.8 %fusion.6 = f32[768,64]{0,1:T(8,128)S(1)} fusion(f32[768,768]{1,0:T(8,128)} %get-tuple-element.64, f32[768,64]{1,0:T(8,128)S(1)} %get-tuple-element.66), kind=kOutput, calls=%fused_computation.24 | convolution fusion | flops 452984832 | bytes 2752512 | tf_op jit(solution)/shard_map/cond/branch_1_fun/dot_general | solution.py:13
  13.9 0.7 broadcast_select_fusion.3
  14.6 1.3 dynamic_slice.13
  17.2 28.1 %all-reduce.8.cloned.1.call-done = f32[768,64]{0,1:T(8,128)} async-done(((f32[768,64]{0,1:T(8,128)}), f32[768,64]{0,1:T(8,128)}) %all-reduce.8.cloned.1.call-update) | async-done | bytes 196624 | tf_op jit(solution)/shard_map/psum | solution.py:9
  45.4 0.9 copy.6
  47.0 37.9 %all-reduce.10.cloned.1.call-done = f32[768,64]{1,0:T(8,128)} async-done(((f32[768,64]{1,0:T(8,128)}), f32[768,64]{1,0:T(8,128)}) %all-reduce.10.cloned.1.call-update) | async-done | bytes 196624 | tf_op jit(solution)/shard_map/psum | solution.py:30
  84.9 0.7 broadcast_select_fusion.2
  86.4 32.2 %all-reduce.12.cloned.1.call-done = f32[768,64]{0,1:T(8,128)} async-done(((f32[768,64]{0,1:T(8,128)}), f32[768,64]{0,1:T(8,128)}) %all-reduce.12.cloned.1.call-update) | async-done | bytes 196624 | tf_op jit(solution)/shard_map/psum | solution.py:9
  118.6 0.9 copy.8
  120.2 38.6 %all-reduce.14.cloned.1.call-done = f32[768,64]{1,0:T(8,128)} async-done(((f32[768,64]{1,0:T(8,128)}), f32[768,64]{1,0:T(8,128)}) %all-reduce.14.cloned.1.call-update) | async-done | bytes 196624 | tf_op jit(solution)/shard_map/psum | solution.py:30
  158.8 1.0 add.71
  159.9 0.7 broadcast_select_fusion.1
  161.3 34.4 %all-reduce.16.cloned.1.call-done = f32[768,64]{0,1:T(8,128)} async-done(((f32[768,64]{0,1:T(8,128)}), f32[768,64]{0,1:T(8,128)}) %all-reduce.16.cloned.1.call-update) | async-done | bytes 196624 | tf_op jit(solution)/shard_map/psum | solution.py:9
  195.7 0.2 conditional.12
  195.9 0.9 copy.10
  197.5 38.1 %all-reduce.18.cloned.1.call-done = f32[768,64]{1,0:T(8,128)} async-done(((f32[768,64]{1,0:T(8,128)}), f32[768,64]{1,0:T(8,128)}) %all-reduce.18.cloned.1.call-update) | async-done | bytes 196624 | tf_op jit(solution)/shard_map/psum | solution.py:30
  235.7 0.7 broadcast_select_fusion
  236.4 32.9 %all-reduce.20.cloned.1.call-done = f32[768,64]{0,1:T(8,128)} async-done(((f32[768,64]{0,1:T(8,128)}), f32[768,64]{0,1:T(8,128)}) %all-reduce.20.cloned.1.call-update) | async-done | bytes 196624 | tf_op jit(solution)/shard_map/psum | solution.py:9
  269.3 1.8 fusion.4
  (32 shorter events, 0.8 us)
Async XLA Ops:
  6.5 38.8 %all-reduce.8.cloned.1.call-start = ((), (), s32[]{:S(2)}) async-start(), calls=%async_computation | async-start | bytes 393216 | tf_op jit(solution)/shard_map/psum | solution.py:9
  14.6 70.3 %all-reduce.10.cloned.1.call-start = ((), (), s32[]{:S(2)}) async-start(), calls=%async_computation.1 | async-start | bytes 786432 | tf_op jit(solution)/shard_map/psum | solution.py:30
  46.3 72.2 %all-reduce.12.cloned.1.call-start = ((), (), s32[]{:S(2)}) async-start(), calls=%async_computation.2 | async-start | bytes 393216 | tf_op jit(solution)/shard_map/psum | solution.py:9
  84.9 73.9 %copy-start = (f32[768,64]{1,0:T(8,128)S(1)}, f32[768,64]{1,0:T(8,128)}, u32[]{:S(2)}) copy-start(f32[768,64]{1,0:T(8,128)} %all-reduce.10.cloned.1.call-done) | copy-start | bytes 589828
  85.7 73.1 %all-reduce.14.cloned.1.call-start = ((), (), s32[]{:S(2)}) async-start(), calls=%async_computation.3 | async-start | bytes 786432 | tf_op jit(solution)/shard_map/psum | solution.py:30
  119.5 76.2 %all-reduce.16.cloned.1.call-start = ((), (), s32[]{:S(2)}) async-start(), calls=%async_computation.4 | async-start | bytes 393216 | tf_op jit(solution)/shard_map/psum | solution.py:9
  160.6 75.0 %all-reduce.18.cloned.1.call-start = ((), (), s32[]{:S(2)}) async-start(), calls=%async_computation.5 | async-start | bytes 786432 | tf_op jit(solution)/shard_map/psum | solution.py:30
  196.9 72.5 %all-reduce.20.cloned.1.call-start = ((), (), s32[]{:S(2)}) async-start(), calls=%async_computation.6 | async-start | bytes 393216 | tf_op jit(solution)/shard_map/psum | solution.py:9
Sparse Core Ops, SparseCore 0:
  14.7 30.5 all-reduce.7
  47.8 37.0 all-reduce.9
  87.2 31.2 all-reduce.11
  120.9 37.8 all-reduce.13
  161.0 34.6 all-reduce.15
  198.0 37.5 all-reduce.17
  238.0 31.2 all-reduce.19
where the time goes:
time: 278 us
  waiting for transfers between devices  242 us (87%)
  between operations  18.7 us (7%)
  other arithmetic  6.79 us (2%)
  local copies, waits for them, and re-layouts  5.85 us (2%)
  matrix products  3.79 us (1%)
    psum x4, waiting for transfers between devices, from_root(): return lax.psum(jnp.where(mine, shard, jnp.zeros_like(shard)), axis)  128 us
    psum x3, waiting for transfers between devices, advance(): carried = carried + lax.psum(product, 'col')  115 us
  transfers between devices with their start and end apart: 7, of which 7 were waited for; matrix products, arithmetic and copies ran while one was open for 0% of the time, Pallas kernels for 0%

commit v1 on v0

--- a/solution.py
+++ b/solution.py
@@ -27,7 +27,7 @@
     arrived = from_root(fresh, "row", lax.axis_index("col"))
     if not final_level:
         product = lax.cond(apply_now, solve_branch, empty_branch, arrived)
-        carried = carried + lax.psum(product, "col")
+        carried = carried + jnp.sum(lax.all_gather(product, "col"), axis=0)
     return (arrived, carried)
 
 

time: 278 us -> 224 us (0.81)
  waiting for transfers between devices: 242 us -> 124 us
  blocking collectives: 0 us -> 57.1 us
  other arithmetic: 6.79 us -> 10.7 us
  local copies, waits for them, and re-layouts: 5.85 us -> 9.15 us
    psum x3 -> x0, waiting for transfers between devices: 115 us -> none  [advance(): carried = carried + lax.psum(product, 'col')]
    all_gather x0 -> x3, blocking collectives: none -> 57.1 us  [advance(): carried = carried + jnp.sum(lax.all_gather(product, 'col'), axis=0)]
    all_gather x0 -> x3, local copies, waits for them, and re-layouts: none -> 4.65 us  [advance(): carried = carried + jnp.sum(lax.all_gather(product, 'col'), axis=0)]
    psum x4, waiting for transfers between devices: 128 us -> 124 us  [from_root(): return lax.psum(jnp.where(mine, shard, jnp.zeros_like(shard)), axis)]
  transfers between devices with their start and end apart: 7 -> 4, of which waited for: 7 -> 4; matrix products, arithmetic and copies ran while one was open for 0% -> 1% of each run, Pallas kernels for 0% -> 0%
where the time goes in v1:
time: 224 us
  waiting for transfers between devices  124 us (55%)
  blocking collectives  57.1 us (25%)
  between operations  18.4 us (8%)
  other arithmetic  10.7 us (5%)
  local copies, waits for them, and re-layouts  9.15 us (4%)
  matrix products  3.79 us (2%)
    psum x4, waiting for transfers between devices, from_root(): return lax.psum(jnp.where(mine, shard, jnp.zeros_like(shard)), axis)  124 us
    all_gather x3, blocking collectives, advance(): carried = carried + jnp.sum(lax.all_gather(product, 'col'), axis=0)  57.1 us
    all_gather x3, local copies, waits for them, and re-layouts, advance(): carried = carried + jnp.sum(lax.all_gather(product, 'col'), axis=0)  4.65 us
  transfers between devices with their start and end apart: 4, of which 4 were waited for; matrix products, arithmetic and copies ran while one was open for 1% of the time, Pallas kernels for 0%

profile of v1, /device:TPU:0, one launch (start us, length us, event | category | flops | bytes accessed | tf_op | source)
XLA Modules:
  0.0 223.5 jit_solution(14867156561466725131)
XLA Ops:
  6.5 0.8 select_reduce_fusion.3
  9.0 1.1 copy.9
  10.1 3.8 %conditional.7 = (f32[768,64]{0,1:T(8,128)S(1)}) conditional(s32[]{:T(128)} %convert_element_type.21, () %tuple.47, (f32[768,768]{1,0:T(8,128)}, f32[768,64]{1,0:T(8,128)S(1)}) %tuple.101), branch_computations={%region_4.5_spmd, %region_5.6_spmd} | conditional | flops 452984832 | bytes 2752520 | solution.py:26
  10.1 3.8 %fusion.6 = f32[768,64]{0,1:T(8,128)S(1)} fusion(f32[768,768]{1,0:T(8,128)} %get-tuple-element.68, f32[768,64]{1,0:T(8,128)S(1)} %get-tuple-element.69), kind=kOutput, calls=%fused_computation.24 | convolution fusion | flops 452984832 | bytes 2752512 | tf_op jit(solution)/shard_map/cond/branch_1_fun/dot_general | solution.py:13
  13.9 0.7 broadcast_select_fusion.3
  14.7 1.3 dynamic_slice.13
  17.9 27.4 %all-reduce.5.cloned.1.call-done = f32[768,64]{0,1:T(8,128)} async-done(((f32[768,64]{0,1:T(8,128)}), f32[768,64]{0,1:T(8,128)}) %all-reduce.5.cloned.1.call-update) | async-done | bytes 196624 | tf_op jit(solution)/shard_map/psum | solution.py:9
  45.4 17.9 %all-gather = f32[3072,64]{0,1:T(8,128)} all-gather(f32[768,64]{0,1:T(8,128)S(1)} %get-tuple-element.113), channel_id=2, replica_groups=mesh['grp'=2,'row'=4,'col'=4] {'col'}, dimensions={0}, use_global_device_ids=true | all-gather | bytes 983040 | tf_op jit(solution)/shard_map/all_gather | solution.py:30
  63.4 1.5 reshape.28
  64.9 1.2 reduce_sum.28
  66.1 0.7 broadcast_select_fusion.2
  68.1 31.9 %all-reduce.7.cloned.1.call-done = f32[768,64]{0,1:T(8,128)} async-done(((f32[768,64]{0,1:T(8,128)}), f32[768,64]{0,1:T(8,128)}) %all-reduce.7.cloned.1.call-update) | async-done | bytes 196624 | tf_op jit(solution)/shard_map/psum | solution.py:9
  100.1 19.4 %all-gather.1 = f32[3072,64]{0,1:T(8,128)} all-gather(f32[768,64]{0,1:T(8,128)S(1)} %get-tuple-element.115), channel_id=3, replica_groups=mesh['grp'=2,'row'=4,'col'=4] {'col'}, dimensions={0}, use_global_device_ids=true | all-gather | bytes 983040 | tf_op jit(solution)/shard_map/all_gather | solution.py:30
  119.5 1.5 reshape.29
  121.0 1.1 reduce_sum.29
  122.1 1.7 add.65
  124.1 0.7 broadcast_select_fusion.1
  126.1 31.9 %all-reduce.9.cloned.1.call-done = f32[768,64]{0,1:T(8,128)} async-done(((f32[768,64]{0,1:T(8,128)}), f32[768,64]{0,1:T(8,128)}) %all-reduce.9.cloned.1.call-update) | async-done | bytes 196624 | tf_op jit(solution)/shard_map/psum | solution.py:9
  158.7 19.7 %all-gather.2 = f32[3072,64]{0,1:T(8,128)S(1)} all-gather(f32[768,64]{0,1:T(8,128)} %copy-done.1), channel_id=4, replica_groups=mesh['grp'=2,'row'=4,'col'=4] {'col'}, dimensions={0}, use_global_device_ids=true | all-gather | bytes 983040 | tf_op jit(solution)/shard_map/all_gather | solution.py:30
  178.4 1.6 copy.15
  180.0 0.7 conditional.13
  180.7 1.6 broadcast_select_fusion
  182.4 32.8 %all-reduce.11.cloned.1.call-done = f32[768,64]{0,1:T(8,128)} async-done(((f32[768,64]{0,1:T(8,128)}), f32[768,64]{0,1:T(8,128)}) %all-reduce.11.cloned.1.call-update) | async-done | bytes 196624 | tf_op jit(solution)/shard_map/psum | solution.py:9
  215.2 1.8 fusion.4
  (30 shorter events, 2.9 us)
Async XLA Ops:
  6.5 38.9 %all-reduce.5.cloned.1.call-start = ((), (), s32[]{:S(2)}) async-start(), calls=%async_computation | async-start | bytes 393216 | tf_op jit(solution)/shard_map/psum | solution.py:9
  14.6 85.4 %all-reduce.7.cloned.1.call-start = ((), (), s32[]{:S(2)}) async-start(), calls=%async_computation.1 | async-start | bytes 393216 | tf_op jit(solution)/shard_map/psum | solution.py:9
  45.4 20.6 %copy-start = (f32[1,1,768,768]{3,2,1,0:T(8,128)S(1)}, f32[1,1,768,768]{3,2,1,0:T(8,128)}, u32[]{:S(2)}) copy-start(f32[1,1,768,768]{3,2,1,0:T(8,128)} %param.17) | copy-start | bytes 7077892
  66.8 91.2 %all-reduce.9.cloned.1.call-start = ((), (), s32[]{:S(2)}) async-start(), calls=%async_computation.2 | async-start | bytes 393216 | tf_op jit(solution)/shard_map/psum | solution.py:9
  124.8 90.4 %all-reduce.11.cloned.1.call-start = ((), (), s32[]{:S(2)}) async-start(), calls=%async_computation.3 | async-start | bytes 393216 | tf_op jit(solution)/shard_map/psum | solution.py:9
  158.0 0.7 copy-start.1
Sparse Core Ops, SparseCore 0:
  14.8 30.5 all-reduce.4
  66.9 33.0 all-reduce.6
  124.9 33.0 all-reduce.8
  182.5 32.6 all-reduce.10
